TPU v7x, 128 devices: a whole 4x4x4 slice. The times are simulated.
128 devices in a mesh: dom: 32 (over y, x, core), near: 4 (over z).
Axes of the slice: x: 4, y: 4, z: 4, core: 2. Of those that a mesh axis runs over, the one named last changes fastest.
Arguments:
- start_block: float32 [131072, 128], P(('dom', 'near')), may hold values from -6 to 6
- near_tiles: float32 [6144, 128, 128], P(('dom', 'near')), may hold values from -0.09375 to 0.09375
- near_src: int32 [6144], P(('dom', 'near')), may hold values from 0 to 31, as said below
- near_mask: int32 [6144], P(('dom', 'near')), may hold values 0 or 1
- far_tiles: float32 [1024, 128, 128], P(('dom', 'near')), may hold values from -0.09375 to 0.09375
- far_src: int32 [1024], P(('dom', 'near')), may hold values from 0 to 31
- far_mask: int32 [1024], P(('dom', 'near')), may hold values 0 or 1
- bound_count: int32 [128], P(('dom', 'near')), may hold values from 1 to 128
Outputs:
- encodings: float32 [131072, 128], P(('dom', 'near'))
- rayleigh: float32 [128, 128], replicated
Inputs may be any that keep to these rules, and one draw needn't show every extreme that they name: `near_src`: each partition holds 48 consecutive slots; the slot at position j among them (j from 0) lies in tile row j // 6; the first slot of each tile row reads the partition's own tile of that row; every source tile from another partition of the group is one of that partition's first 4 tiles.
All inputs are finite; a program needn't handle non-finite values. No bound on the sum of `near_mask` or of `far_mask` on one device may be relied on, other than what follows from the above.
Results may differ from a plain program's by a relative error of at most 0.0003.
Values sent between devices are 32-bit elements; how exact they have to be, the bound alone decides.
No kernel may reach another device: no remote copies, remote signals or barrier semaphores. Data moves between devices by JAX's collectives and lax.ppermute only.
A program may use at most 64 MiB of HBM per device.

v0:
```python
from functools import partial
import jax
import jax.numpy as jnp
from jax import lax
from jax.sharding import PartitionSpec as P

NPER = 6
ITERS = 2
DEG = 3
LOWER_EDGE = 0.6
UPPER_EDGE = 2.0


def apply_operator(
    block, near_tiles, near_src, near_mask, far_tiles, far_src, far_mask, bound_count
):
    tile_rows = near_tiles.shape[1]
    width = block.shape[1]
    tiles_dev = block.shape[0] // tile_rows
    group_size = lax.axis_size("near")
    gathered = lax.all_gather(block, "near", axis=0, tiled=True)
    picked = gathered.reshape(group_size * tiles_dev, tile_rows, width)[near_src]
    products = jnp.einsum("sij,sjk->sik", near_tiles, picked, precision=lax.Precision.HIGHEST)
    products = products * near_mask.astype(jnp.float32)[:, None, None]
    near_sum = products.reshape(tiles_dev, NPER, tile_rows, width).sum(axis=1)
    limit = (jnp.arange(tile_rows) < bound_count[0]).astype(jnp.float32)
    edge_tile = block[:tile_rows] * limit[:, None]
    edges = lax.all_gather(edge_tile, "dom", axis=0, tiled=True).reshape(
        lax.axis_size("dom"), tile_rows, width
    )
    far_pick = edges[far_src]
    far_sum = jnp.einsum("sij,sjk->sik", far_tiles, far_pick, precision=lax.Precision.HIGHEST)
    far_sum = far_sum * far_mask.astype(jnp.float32)[:, None, None]
    return block - (near_sum + far_sum).reshape(block.shape)


def chebyshev(current, image, operator):
    center = (UPPER_EDGE + LOWER_EDGE) / 2.0
    half = (UPPER_EDGE - LOWER_EDGE) / 2.0
    previous = current
    present = (image - center * current) / half
    for degree in range(DEG - 1):
        following = 2.0 * (operator(present) - center * present) / half - previous
        previous, present = (present, following)
    return present


def inner(left, right):
    return jnp.dot(
        left.T, right, precision=lax.Precision.HIGHEST, preferred_element_type=jnp.float32
    )


def times_inverse(block, lower_inv):
    return jnp.dot(
        block, lower_inv.T, precision=lax.Precision.HIGHEST, preferred_element_type=jnp.float32
    )


def inverse_factor(gram):
    lower = jnp.linalg.cholesky(gram)
    return jax.scipy.linalg.solve_triangular(
        lower, jnp.eye(gram.shape[0], dtype=jnp.float32), lower=True
    )


def local(start_block, near_tiles, near_src, near_mask, far_tiles, far_src, far_mask, bound_count):
    operator = partial(
        apply_operator,
        near_tiles=near_tiles,
        near_src=near_src,
        near_mask=near_mask,
        far_tiles=far_tiles,
        far_src=far_src,
        far_mask=far_mask,
        bound_count=bound_count,
    )
    nodes_all = start_block.shape[0] * lax.axis_size("dom") * lax.axis_size("near")
    current = start_block
    image = operator(current)
    for iteration in range(ITERS):
        if iteration > 0:
            image = operator(current)
        filtered = chebyshev(current, image, operator)
        gram = lax.psum(inner(filtered, filtered), ("dom", "near")) / nodes_all
        lower_inv = inverse_factor(gram)
        current = times_inverse(filtered, lower_inv)
    final_image = operator(current)
    rayleigh = lax.psum(inner(current, final_image), ("dom", "near")) / nodes_all
    return (current, rayleigh)


def solution(mesh):
    return jax.shard_map(
        local,
        mesh=mesh,
        in_specs=(
            P(("dom", "near"), None),
            P(("dom", "near"), None, None),
            P(("dom", "near")),
            P(("dom", "near")),
            P(("dom", "near"), None, None),
            P(("dom", "near")),
            P(("dom", "near")),
            P(("dom", "near")),
        ),
        out_specs=(P(("dom", "near"), None), P()),
        check_vma=False,
    )
```

profile of v0, /device:TPU:1, one launch (start us, length us, event | category | flops | bytes accessed | tf_op | source)
XLA Modules:
  0.0 1082.7 jit_solution(1137057290617790462)
XLA Ops:
  13.1 30.7 %all-gather.15.cloned.1.call-done = f32[4096,128]{1,0:T(8,128)} async-done(((f32[1024,128]{1,0:T(8,128)}), f32[4096,128]{1,0:T(8,128)}) %all-gather.15.cloned.1.call-update) | async-done | bytes 2097168 | tf_op jit(solution)/shard_map/all_gather | solution.py:21
  43.7 4.0 gather_fusion
  47.7 8.1 convolution_multiply_fusion.6
  60.8 29.6 %all-gather.17.cloned.1.call-done = f32[4096,128]{1,0:T(8,128)} async-done(((f32[128,128]{1,0:T(8,128)}), f32[4096,128]{1,0:T(8,128)}) %all-gather.17.cloned.1.call-update) | async-done | bytes 2097168 | tf_op jit(solution)/shard_map/all_gather | solution.py:28
  99.8 28.3 %all-gather.19.cloned.1.call-done = f32[4096,128]{1,0:T(8,128)} async-done(((f32[1024,128]{1,0:T(8,128)}), f32[4096,128]{1,0:T(8,128)}) %all-gather.19.cloned.1.call-update) | async-done | bytes 2097168 | tf_op jit(solution)/shard_map/all_gather | solution.py:21
  128.1 4.0 gather_fusion.2
  132.1 8.1 convolution_multiply_fusion.5
  145.2 29.5 %all-gather.21.cloned.1.call-done = f32[4096,128]{1,0:T(8,128)} async-done(((f32[128,128]{1,0:T(8,128)}), f32[4096,128]{1,0:T(8,128)}) %all-gather.21.cloned.1.call-update) | async-done | bytes 2097168 | tf_op jit(solution)/shard_map/all_gather | solution.py:28
  184.5 28.1 %all-gather.23.cloned.1.call-done = f32[4096,128]{1,0:T(8,128)} async-done(((f32[1024,128]{1,0:T(8,128)}), f32[4096,128]{1,0:T(8,128)}) %all-gather.23.cloned.1.call-update) | async-done | bytes 2097168 | tf_op jit(solution)/shard_map/all_gather | solution.py:21
  212.6 4.0 gather_fusion.4
  216.5 8.1 convolution_multiply_fusion.4
  229.7 29.5 %all-gather.25.cloned.1.call-done = f32[4096,128]{1,0:T(8,128)} async-done(((f32[128,128]{1,0:T(8,128)}), f32[4096,128]{1,0:T(8,128)}) %all-gather.25.cloned.1.call-update) | async-done | bytes 2097168 | tf_op jit(solution)/shard_map/all_gather | solution.py:28
  268.2 138.8 %all-reduce.4.cloned.1.call-done = f32[128,128]{0,1:T(8,128)} async-done(((f32[128,128]{0,1:T(8,128)}), f32[128,128]{0,1:T(8,128)}) %all-reduce.4.cloned.1.call-update) | async-done | bytes 65552 | tf_op jit(solution)/shard_map/psum | solution.py:85
  408.8 11.7 %cholesky.44 = f32[128,128]{1,0:T(8,128)S(1)} custom-call(f32[128,128]{1,0:T(8,128)S(1)} %fusion.41), custom_call_target="Cholesky" | custom-call | tf_op jit(solution)/shard_map/jit(cholesky)/cholesky | solution.py:61
  421.9 9.8 custom-call.6
  436.1 26.2 %all-gather.27.cloned.1.call-done = f32[4096,128]{1,0:T(8,128)} async-done(((f32[1024,128]{1,0:T(8,128)}), f32[4096,128]{1,0:T(8,128)}) %all-gather.27.cloned.1.call-update) | async-done | bytes 2097168 | tf_op jit(solution)/shard_map/all_gather | solution.py:21
  462.3 4.0 gather_fusion.6
  466.3 8.1 convolution_multiply_fusion.3
  479.4 29.6 %all-gather.29.cloned.1.call-done = f32[4096,128]{1,0:T(8,128)} async-done(((f32[128,128]{1,0:T(8,128)}), f32[4096,128]{1,0:T(8,128)}) %all-gather.29.cloned.1.call-update) | async-done | bytes 2097168 | tf_op jit(solution)/shard_map/all_gather | solution.py:28
  518.6 28.1 %all-gather.31.cloned.1.call-done = f32[4096,128]{1,0:T(8,128)} async-done(((f32[1024,128]{1,0:T(8,128)}), f32[4096,128]{1,0:T(8,128)}) %all-gather.31.cloned.1.call-update) | async-done | bytes 2097168 | tf_op jit(solution)/shard_map/all_gather | solution.py:21
  550.7 8.1 convolution_multiply_fusion.2
  563.8 29.6 %all-gather.33.cloned.1.call-done = f32[4096,128]{1,0:T(8,128)} async-done(((f32[128,128]{1,0:T(8,128)}), f32[4096,128]{1,0:T(8,128)}) %all-gather.33.cloned.1.call-update) | async-done | bytes 2097168 | tf_op jit(solution)/shard_map/all_gather | solution.py:28
  603.0 28.3 %all-gather.35.cloned.1.call-done = f32[4096,128]{1,0:T(8,128)} async-done(((f32[1024,128]{1,0:T(8,128)}), f32[4096,128]{1,0:T(8,128)}) %all-gather.35.cloned.1.call-update) | async-done | bytes 2097168 | tf_op jit(solution)/shard_map/all_gather | solution.py:21
  635.3 8.1 convolution_multiply_fusion.1
  648.4 29.6 %all-gather.37.cloned.1.call-done = f32[4096,128]{1,0:T(8,128)} async-done(((f32[128,128]{1,0:T(8,128)}), f32[4096,128]{1,0:T(8,128)}) %all-gather.37.cloned.1.call-update) | async-done | bytes 2097168 | tf_op jit(solution)/shard_map/all_gather | solution.py:28
  687.5 138.4 %all-reduce.6.cloned.1.call-done = f32[128,128]{0,1:T(8,128)} async-done(((f32[128,128]{0,1:T(8,128)}), f32[128,128]{0,1:T(8,128)}) %all-reduce.6.cloned.1.call-update) | async-done | bytes 65552 | tf_op jit(solution)/shard_map/psum | solution.py:85
  827.7 11.7 %cholesky.55 = f32[128,128]{1,0:T(8,128)S(1)} custom-call(f32[128,128]{1,0:T(8,128)S(1)} %fusion.39), custom_call_target="Cholesky" | custom-call | tf_op jit(solution)/shard_map/jit(cholesky)/cholesky | solution.py:61
  840.8 9.8 custom-call.7
  855.2 26.0 %all-gather.39.cloned.1.call-done = f32[4096,128]{1,0:T(8,128)} async-done(((f32[1024,128]{1,0:T(8,128)}), f32[4096,128]{1,0:T(8,128)}) %all-gather.39.cloned.1.call-update) | async-done | bytes 2097168 | tf_op jit(solution)/shard_map/all_gather | solution.py:21
  885.2 8.1 convolution_multiply_fusion
  898.3 29.5 %all-gather.41.cloned.1.call-done = f32[4096,128]{1,0:T(8,128)} async-done(((f32[128,128]{1,0:T(8,128)}), f32[4096,128]{1,0:T(8,128)}) %all-gather.41.cloned.1.call-update) | async-done | bytes 2097168 | tf_op jit(solution)/shard_map/all_gather | solution.py:28
  935.5 138.9 %all-reduce.8.cloned.1.call-done = f32[128,128]{0,1:T(8,128)} async-done(((f32[128,128]{0,1:T(8,128)}), f32[128,128]{0,1:T(8,128)}) %all-reduce.8.cloned.1.call-update) | async-done | bytes 65552 | tf_op jit(solution)/shard_map/psum | solution.py:89
  (120 shorter events, 133.1 us)
Async XLA Ops:
  7.2 40.5 %copy-start = (f32[48,128,128]{2,1,0:T(8,128)S(1)}, f32[48,128,128]{2,1,0:T(8,128)}, u32[]{:S(2)}) copy-start(f32[48,128,128]{2,1,0:T(8,128)} %param.12) | copy-start | bytes 9437188
  7.2 36.5 %all-gather.15.cloned.1.call-start = ((), (), s32[]{:S(2)}) async-start(), calls=%async_computation | async-start | bytes 2621440 | tf_op jit(solution)/shard_map/all_gather | solution.py:21
  7.9 82.5 %all-gather.17.cloned.1.call-start = ((), (), s32[]{:S(2)}) async-start(), calls=%async_computation.1 | async-start | bytes 2162688 | tf_op jit(solution)/shard_map/all_gather | solution.py:28
  10.4 117.7 %all-gather.19.cloned.1.call-start = ((), (), s32[]{:S(2)}) async-start(), calls=%async_computation.2 | async-start | bytes 2621440 | tf_op jit(solution)/shard_map/all_gather | solution.py:21
  95.4 0.8 copy-start.2
  98.1 76.5 %all-gather.21.cloned.1.call-start = ((), (), s32[]{:S(2)}) async-start(), calls=%async_computation.3 | async-start | bytes 2162688 | tf_op jit(solution)/shard_map/all_gather | solution.py:28
  99.8 112.8 %all-gather.23.cloned.1.call-start = ((), (), s32[]{:S(2)}) async-start(), calls=%async_computation.4 | async-start | bytes 2621440 | tf_op jit(solution)/shard_map/all_gather | solution.py:21
  179.6 0.8 copy-start.6
  182.6 76.5 %all-gather.25.cloned.1.call-start = ((), (), s32[]{:S(2)}) async-start(), calls=%async_computation.5 | async-start | bytes 2162688 | tf_op jit(solution)/shard_map/all_gather | solution.py:28
  184.2 222.8 %all-reduce.4.cloned.1.call-start = ((), (), s32[]{:S(2)}) async-start(), calls=%async_computation.6 | async-start | bytes 131072 | tf_op jit(solution)/shard_map/psum | solution.py:85
  265.7 0.8 copy-start.4
  268.1 194.2 %all-gather.27.cloned.1.call-start = ((), (), s32[]{:S(2)}) async-start(), calls=%async_computation.7 | async-start | bytes 2621440 | tf_op jit(solution)/shard_map/all_gather | solution.py:21
  434.5 74.6 %all-gather.29.cloned.1.call-start = ((), (), s32[]{:S(2)}) async-start(), calls=%async_computation.8 | async-start | bytes 2162688 | tf_op jit(solution)/shard_map/all_gather | solution.py:28
  436.1 110.6 %all-gather.31.cloned.1.call-start = ((), (), s32[]{:S(2)}) async-start(), calls=%async_computation.9 | async-start | bytes 2621440 | tf_op jit(solution)/shard_map/all_gather | solution.py:21
  514.0 0.8 copy-start.1
  516.7 76.7 %all-gather.33.cloned.1.call-start = ((), (), s32[]{:S(2)}) async-start(), calls=%async_computation.10 | async-start | bytes 2162688 | tf_op jit(solution)/shard_map/all_gather | solution.py:28
  518.4 112.9 %all-gather.35.cloned.1.call-start = ((), (), s32[]{:S(2)}) async-start(), calls=%async_computation.11 | async-start | bytes 2621440 | tf_op jit(solution)/shard_map/all_gather | solution.py:21
  598.3 0.8 copy-start.5
  601.3 76.7 %all-gather.37.cloned.1.call-start = ((), (), s32[]{:S(2)}) async-start(), calls=%async_computation.12 | async-start | bytes 2162688 | tf_op jit(solution)/shard_map/all_gather | solution.py:28
  603.0 223.0 %all-reduce.6.cloned.1.call-start = ((), (), s32[]{:S(2)}) async-start(), calls=%async_computation.13 | async-start | bytes 131072 | tf_op jit(solution)/shard_map/psum | solution.py:85
  684.6 0.8 copy-start.3
  687.0 194.1 %all-gather.39.cloned.1.call-start = ((), (), s32[]{:S(2)}) async-start(), calls=%async_computation.14 | async-start | bytes 2621440 | tf_op jit(solution)/shard_map/all_gather | solution.py:21
  853.3 74.4 %all-gather.41.cloned.1.call-start = ((), (), s32[]{:S(2)}) async-start(), calls=%async_computation.15 | async-start | bytes 2162688 | tf_op jit(solution)/shard_map/all_gather | solution.py:28
  855.0 219.5 %all-reduce.8.cloned.1.call-start = ((), (), s32[]{:S(2)}) async-start(), calls=%async_computation.16 | async-start | bytes 131072 | tf_op jit(solution)/shard_map/psum | solution.py:89
Sparse Core Ops, SparseCore 0:
  9.6 34.0 all-gather.14
  46.5 43.8 all-gather.16
  98.3 29.7 all-gather.18
  130.8 43.8 all-gather.20
  182.7 29.7 all-gather.22
  215.2 43.8 all-gather.24
  268.3 138.7 all-reduce.3
  434.6 27.6 all-gather.26
  465.1 43.8 all-gather.28
  516.9 29.7 all-gather.30
  549.5 43.8 all-gather.32
  601.5 29.7 all-gather.34
  634.1 43.8 all-gather.36
  687.1 138.7 all-reduce.5
  853.4 27.6 all-gather.38
  883.9 43.8 all-gather.40
  935.7 138.7 all-reduce.7
where the time goes:
time: 1090 us; the launch traced here: 1080 us
  waiting for transfers between devices  819 us (75%)
  other arithmetic  95.5 us (9%)
  matrix products  82.2 us (8%)
  local copies, waits for them, and re-layouts  68.7 us (6%)
  between operations  15.2 us (1%)
    psum x2, waiting for transfers between devices, local(): gram = lax.psum(inner(filtered, filtered), ('dom', 'near')) / nodes_all  277 us
    all_gather x7, waiting for transfers between devices, apply_operator(): lax.all_gather(edge_tile, 'dom', axis=0, tiled=True)  207 us
    all_gather x7, waiting for transfers between devices, apply_operator(): gathered = lax.all_gather(block, 'near', axis=0, tiled=True)  196 us
    psum x1, waiting for transfers between devices, local(): lax.psum(inner(current, final_image), ('dom', 'near')) / nodes_all  139 us
    dot_general x7, matrix products, apply_operator(): jnp.einsum('sij,sjk->sik', near_tiles, picked, precision=lax.Precision.HI...  56.9 us
    gather x7, local copies, waits for them, and re-layouts, apply_operator(): gathered.reshape(group_size * tiles_dev, tile_rows, width)[near_src]  28 us
    another operation x6, other arithmetic, inverse_factor(): lower = jnp.linalg.cholesky(gram)  24.8 us
  transfers between devices with their start and end apart: 17, of which 17 were waited for; matrix products, arithmetic and copies ran while one was open for 12% of the time, Pallas kernels for 0%

commit v1 on v0

--- a/solution.py
+++ b/solution.py
@@ -18,7 +18,9 @@
     width = block.shape[1]
     tiles_dev = block.shape[0] // tile_rows
     group_size = lax.axis_size("near")
-    gathered = lax.all_gather(block, "near", axis=0, tiled=True)
+    gathered = jnp.concatenate(
+        lax.all_to_all(jnp.stack([block] * lax.axis_size("near")), "near", 0, 0), axis=0
+    )
     picked = gathered.reshape(group_size * tiles_dev, tile_rows, width)[near_src]
     products = jnp.einsum("sij,sjk->sik", near_tiles, picked, precision=lax.Precision.HIGHEST)
     products = products * near_mask.astype(jnp.float32)[:, None, None]

time: 1090 us -> 895 us (0.82)
  waiting for transfers between devices: 819 us -> 443 us
  blocking collectives: 0 us -> 172 us
  local copies, waits for them, and re-layouts: 68.7 us -> 83.2 us
  other arithmetic: 95.5 us -> 84.6 us
    all_gather x7, waiting for transfers between devices: 207 us -> 0.68 us  [apply_operator(): lax.all_gather(edge_tile, 'dom', axis=0, tiled=True)]
    all_gather x7 -> x0, waiting for transfers between devices: 196 us -> none  [apply_operator(): gathered = lax.all_gather(block, 'near', axis=0, tiled=True)]
    all_to_all x0 -> x6, blocking collectives: none -> 172 us  [apply_operator(): lax.all_to_all(jnp.stack([block] * lax.axis_size('near')), 'near', 0, 0)]
    all_to_all x0 -> x1, waiting for transfers between devices: none -> 25.6 us  [apply_operator(): lax.all_to_all(jnp.stack([block] * lax.axis_size('near')), 'near', 0, 0)]
  transfers between devices with their start and end apart: 17 -> 11, of which waited for: 17 -> 5; matrix products, arithmetic and copies ran while one was open for 12% -> 15% of each run, Pallas kernels for 0% -> 0%
where the time goes in v1:
time: 895 us; the launch traced here: 886 us
  waiting for transfers between devices  443 us (49%)
  blocking collectives  172 us (19%)
  other arithmetic  84.6 us (9%)
  local copies, waits for them, and re-layouts  83.2 us (9%)
  matrix products  80.6 us (9%)
  between operations  15.6 us (2%)
    psum x2, waiting for transfers between devices, local(): gram = lax.psum(inner(filtered, filtered), ('dom', 'near')) / nodes_all  280 us
    all_to_all x6, blocking collectives, apply_operator(): lax.all_to_all(jnp.stack([block] * lax.axis_size('near')), 'near', 0, 0)  172 us
    psum x1, waiting for transfers between devices, local(): lax.psum(inner(current, final_image), ('dom', 'near')) / nodes_all  137 us
    dot_general x7, matrix products, apply_operator(): jnp.einsum('sij,sjk->sik', near_tiles, picked, precision=lax.Precision.HI...  57 us
    gather x7, local copies, waits for them, and re-layouts, apply_operator(): gathered.reshape(group_size * tiles_dev, tile_rows, width)[near_src]  28.2 us
    all_to_all x1, waiting for transfers between devices, apply_operator(): lax.all_to_all(jnp.stack([block] * lax.axis_size('near')), 'near', 0, 0)  25.6 us
    another operation x6, other arithmetic, inverse_factor(): lower = jnp.linalg.cholesky(gram)  24.8 us
    another operation x4, other arithmetic, inverse_factor(): jax.scipy.linalg.solve_triangular(lower, jnp.eye(gram.shape[0], dtype=jnp...  20.9 us
  transfers between devices with their start and end apart: 11, of which 5 were waited for; matrix products, arithmetic and copies ran while one was open for 15% of the time, Pallas kernels for 0%

profile of v1, /device:TPU:1, one launch (start us, length us, event | category | flops | bytes accessed | tf_op | source)
XLA Modules:
  0.0 885.5 jit_solution(9739032829857342535)
XLA Ops:
  12.3 5.8 all-to-all-start
  18.2 25.6 %all-to-all-done = f32[4,1024,128]{2,1,0:T(8,128)} async-done(((f32[4,1024,128]{2,1,0:T(8,128)}), f32[4,1024,128]{2,1,0:T(8,128)}, u32[]{:S(2)}, u32[]{:S(2)}) %all-to-all-start) | async-done | bytes 2097184 | tf_op jit(solution)/shard_map/all_to_all | solution.py:22
  43.8 4.0 gather_fusion
  47.8 8.1 convolution_multiply_fusion.6
  60.9 3.0 gather_fusion.1
  70.5 27.8 %all_to_all.35 = f32[4,1024,128]{2,1,0:T(8,128)} all-to-all(f32[4,1024,128]{2,1,0:T(8,128)S(1)} %stack.15), channel_id=1, replica_groups=mesh['dom'=32,'near'=4] {'near'}, dimensions={0} | all-to-all | bytes 4194304 | tf_op jit(solution)/shard_map/all_to_all | solution.py:22
  98.3 4.0 gather_fusion.2
  102.3 8.1 convolution_multiply_fusion.5
  115.4 3.0 gather_fusion.3
  125.3 26.7 %all_to_all.36 = f32[4,1024,128]{2,1,0:T(8,128)} all-to-all(f32[4,1024,128]{2,1,0:T(8,128)S(1)} %stack.16), channel_id=1, replica_groups=mesh['dom'=32,'near'=4] {'near'}, dimensions={0} | all-to-all | bytes 4194304 | tf_op jit(solution)/shard_map/all_to_all | solution.py:22
  152.0 4.0 gather_fusion.4
  156.0 8.1 convolution_multiply_fusion.4
  169.8 3.0 gather_fusion.5
  178.8 142.0 %all-reduce.4.cloned.1.call-done = f32[128,128]{0,1:T(8,128)} async-done(((f32[128,128]{0,1:T(8,128)}), f32[128,128]{0,1:T(8,128)}) %all-reduce.4.cloned.1.call-update) | async-done | bytes 65552 | tf_op jit(solution)/shard_map/psum | solution.py:87
  322.6 11.7 %cholesky.44 = f32[128,128]{1,0:T(8,128)S(1)} custom-call(f32[128,128]{1,0:T(8,128)S(1)} %fusion.41), custom_call_target="Cholesky" | custom-call | tf_op jit(solution)/shard_map/jit(cholesky)/cholesky | solution.py:63
  335.6 9.8 %custom-call.6 = f32[1,128,128]{1,2,0:T(8,128)S(1)} custom-call(f32[1,128,128]{2,1,0:T(8,128)S(1)} %fusion.36), custom_call_target="InvertDiagBlocksLowerTriangular" | custom-call | tf_op jit(solution)/shard_map/jit(_solve_triangular)/triangular_solve | solution.py:64
  350.1 29.5 %all_to_all.37 = f32[4,1024,128]{2,1,0:T(8,128)} all-to-all(f32[4,1024,128]{2,1,0:T(8,128)S(1)} %stack.17), channel_id=1, replica_groups=mesh['dom'=32,'near'=4] {'near'}, dimensions={0} | all-to-all | bytes 4194304 | tf_op jit(solution)/shard_map/all_to_all | solution.py:22
  379.7 4.1 gather_fusion.6
  383.7 8.2 convolution_multiply_fusion.3
  406.5 29.6 %all_to_all.38 = f32[4,1024,128]{2,1,0:T(8,128)} all-to-all(f32[4,1024,128]{2,1,0:T(8,128)S(1)} %stack.18), channel_id=1, replica_groups=mesh['dom'=32,'near'=4] {'near'}, dimensions={0} | all-to-all | bytes 4194304 | tf_op jit(solution)/shard_map/all_to_all | solution.py:22
  436.1 4.1 gather_fusion.8
  440.2 8.2 convolution_multiply_fusion.2
  463.2 28.6 %all_to_all.39 = f32[4,1024,128]{2,1,0:T(8,128)} all-to-all(f32[4,1024,128]{2,1,0:T(8,128)S(1)} %stack.19), channel_id=1, replica_groups=mesh['dom'=32,'near'=4] {'near'}, dimensions={0} | all-to-all | bytes 4194304 | tf_op jit(solution)/shard_map/all_to_all | solution.py:22
  491.8 4.0 gather_fusion.10
  495.8 8.1 convolution_multiply_fusion.1
  518.3 137.8 %all-reduce.6.cloned.1.call-done = f32[128,128]{0,1:T(8,128)} async-done(((f32[128,128]{0,1:T(8,128)}), f32[128,128]{0,1:T(8,128)}) %all-reduce.6.cloned.1.call-update) | async-done | bytes 65552 | tf_op jit(solution)/shard_map/psum | solution.py:87
  657.9 11.7 %cholesky.55 = f32[128,128]{1,0:T(8,128)S(1)} custom-call(f32[128,128]{1,0:T(8,128)S(1)} %fusion.39), custom_call_target="Cholesky" | custom-call | tf_op jit(solution)/shard_map/jit(cholesky)/cholesky | solution.py:63
  670.9 9.8 %custom-call.7 = f32[1,128,128]{1,2,0:T(8,128)S(1)} custom-call(f32[1,128,128]{2,1,0:T(8,128)S(1)} %fusion.37), custom_call_target="InvertDiagBlocksLowerTriangular" | custom-call | tf_op jit(solution)/shard_map/jit(_solve_triangular)/triangular_solve | solution.py:64
  685.4 29.7 %all_to_all.40 = f32[4,1024,128]{2,1,0:T(8,128)} all-to-all(f32[4,1024,128]{2,1,0:T(8,128)S(1)} %stack.20), channel_id=1, replica_groups=mesh['dom'=32,'near'=4] {'near'}, dimensions={0} | all-to-all | bytes 4194304 | tf_op jit(solution)/shard_map/all_to_all | solution.py:22
  715.1 4.1 gather_fusion.12
  719.2 8.2 convolution_multiply_fusion
  740.1 136.8 %all-reduce.8.cloned.1.call-done = f32[128,128]{0,1:T(8,128)} async-done(((f32[128,128]{0,1:T(8,128)}), f32[128,128]{0,1:T(8,128)}) %all-reduce.8.cloned.1.call-update) | async-done | bytes 65552 | tf_op jit(solution)/shard_map/psum | solution.py:91
  (134 shorter events, 113.0 us)
Async XLA Ops:
  7.2 40.6 %copy-start = (f32[48,128,128]{2,1,0:T(8,128)S(1)}, f32[48,128,128]{2,1,0:T(8,128)}, u32[]{:S(2)}) copy-start(f32[48,128,128]{2,1,0:T(8,128)} %param.12) | copy-start | bytes 9437188
  7.2 53.7 %all-gather.8.cloned.1.call-start = ((), (), s32[]{:S(2)}) async-start(), calls=%async_computation.7 | async-start | bytes 2162688 | tf_op jit(solution)/shard_map/all_gather | solution.py:30
  9.7 8.4 copy-start.13
  9.7 8.4 copy-start.14
  9.7 8.4 copy-start.15
  9.7 8.5 copy-start.16
  12.3 31.5 %all-to-all-start = ((f32[4,1024,128]{2,1,0:T(8,128)}), f32[4,1024,128]{2,1,0:T(8,128)}, u32[]{:S(2)}, u32[]{:S(2)}) async-start(f32[4,1024,128]{2,1,0:T(8,128)} %stack.14), calls=%async_computation | async-start | bytes 4194304 | tf_op jit(solution)/shard_map/all_to_all | solution.py:22
  18.1 97.2 %all-gather.10.cloned.1.call-start = ((), (), s32[]{:S(2)}) async-start(), calls=%async_computation.8 | async-start | bytes 2162688 | tf_op jit(solution)/shard_map/all_gather | solution.py:30
  65.8 0.8 copy-start.4
  67.8 0.8 copy-start.9
  69.3 100.4 %all-gather.12.cloned.1.call-start = ((), (), s32[]{:S(2)}) async-start(), calls=%async_computation.9 | async-start | bytes 2162688 | tf_op jit(solution)/shard_map/all_gather | solution.py:30
  120.3 0.8 copy-start.8
  122.5 0.8 copy-start.11
  124.1 196.7 %all-reduce.4.cloned.1.call-start = ((), (), s32[]{:S(2)}) async-start(), calls=%async_computation.10 | async-start | bytes 131072 | tf_op jit(solution)/shard_map/psum | solution.py:87
  176.3 0.8 copy-start.6
  178.8 218.1 %all-gather.14.cloned.1.call-start = ((), (), s32[]{:S(2)}) async-start(), calls=%async_computation.11 | async-start | bytes 2162688 | tf_op jit(solution)/shard_map/all_gather | solution.py:30
  347.4 0.8 copy-start.1
  348.9 104.4 %all-gather.16.cloned.1.call-start = ((), (), s32[]{:S(2)}) async-start(), calls=%async_computation.12 | async-start | bytes 2162688 | tf_op jit(solution)/shard_map/all_gather | solution.py:30
  401.8 0.8 copy-start.3
  403.8 0.8 copy-start.10
  405.3 103.5 %all-gather.18.cloned.1.call-start = ((), (), s32[]{:S(2)}) async-start(), calls=%async_computation.13 | async-start | bytes 2162688 | tf_op jit(solution)/shard_map/all_gather | solution.py:30
  458.3 0.8 copy-start.7
  460.5 0.8 copy-start.12
  462.0 194.1 %all-reduce.6.cloned.1.call-start = ((), (), s32[]{:S(2)}) async-start(), calls=%async_computation.14 | async-start | bytes 131072 | tf_op jit(solution)/shard_map/psum | solution.py:87
  515.4 0.8 copy-start.5
  517.8 214.5 %all-gather.20.cloned.1.call-start = ((), (), s32[]{:S(2)}) async-start(), calls=%async_computation.15 | async-start | bytes 2162688 | tf_op jit(solution)/shard_map/all_gather | solution.py:30
  682.7 0.8 copy-start.2
  684.2 192.7 %all-reduce.8.cloned.1.call-start = ((), (), s32[]{:S(2)}) async-start(), calls=%async_computation.16 | async-start | bytes 131072 | tf_op jit(solution)/shard_map/psum | solution.py:91
Sparse Core Ops, SparseCore 0:
  10.8 47.0 all-gather.7
  69.4 44.3 all-gather.9
  124.2 45.5 all-gather.11
  178.9 141.8 all-reduce.3
  349.0 40.6 all-gather.13
  405.4 40.6 all-gather.15
  462.1 41.1 all-gather.17
  517.9 138.0 all-reduce.5
  684.3 40.6 all-gather.19
  740.2 136.6 all-reduce.7
